TPU v7x, 512 devices: a whole 4x8x8 slice. The times are simulated.
512 devices in a mesh: ctx: 64 (over x, y, core), tp: 8 (over z).
Axes of the slice: x: 4, y: 8, z: 8, core: 2. Of those that a mesh axis runs over, the one named last changes fastest.
Arguments:
- queries: bfloat16 [32768, 2048], P('ctx', 'tp'), may hold values from -1.75 to 1.75
- keys: bfloat16 [32768, 2048], P('ctx', 'tp'), may hold values from -1.75 to 1.75
- values: bfloat16 [32768, 2048], P('ctx', 'tp'), may hold values from -18 to 18
- gain: bfloat16 [2048], P('tp'), may hold values from 0.099609375 to 1.8984375
- cotangent: bfloat16 [32768, 2048], P('ctx', 'tp'), may hold values from -6 to 6
Outputs:
- normed: bfloat16 [32768, 2048], P('ctx', 'tp')
- grad_queries: bfloat16 [32768, 2048], P('ctx', 'tp')
- grad_keys: bfloat16 [32768, 2048], P('ctx', 'tp')
- grad_values: bfloat16 [32768, 2048], P('ctx', 'tp')
All inputs are finite; a program needn't handle non-finite values.
Results may differ from a plain program's by a relative error of at most 0.0058.
Values sent between devices are 32-bit elements; how exact they have to be, the bound alone decides.
A program may use at most 64 MiB of HBM per device.

v0:
```python
import jax
import jax.numpy as jnp
from jax import lax
from jax.sharding import PartitionSpec as P

HEAD = 128
HEADS = 16
epsilon = 1e-06


def heads_first(matrix, head_count):
    return matrix.reshape(matrix.shape[0], head_count, HEAD).transpose(1, 0, 2)


def heads_last(tensor):
    return tensor.transpose(1, 0, 2).reshape(tensor.shape[1], -1)


def shards(queries, keys, values, gain, cotangent):
    row_count = queries.shape[0]
    head_count = queries.shape[1] // HEAD
    query_heads = heads_first(queries, head_count)
    key_heads = heads_first(keys, head_count)
    value_heads = heads_first(values, head_count)
    causal = jnp.tril(jnp.ones((row_count, row_count), jnp.bool_))
    gain_wide = gain.astype(jnp.float32)
    own_state = jnp.einsum(
        "hte,htf->hef", key_heads, value_heads, preferred_element_type=jnp.float32
    )
    position = lax.axis_index("ctx")
    pieces = lax.all_gather(own_state[None], "ctx", axis=0, tiled=True)
    shard_index = jnp.arange(pieces.shape[0], dtype=jnp.int32)
    lower_mask = (shard_index < position).astype(jnp.float32)
    prior_state = jnp.sum(pieces * lower_mask[:, None, None, None], axis=0)
    prior_low = prior_state.astype(jnp.bfloat16)

    def forward_head(members):
        query_now, key_now, value_now, prior_now = members
        scores = jnp.einsum("te,se->ts", query_now, key_now, preferred_element_type=jnp.float32)
        masked = jnp.where(causal, scores, 0.0).astype(jnp.bfloat16)
        combined = jnp.dot(masked, value_now, preferred_element_type=jnp.float32)
        combined = combined + jnp.dot(query_now, prior_now, preferred_element_type=jnp.float32)
        return (masked, combined)

    masked, combined = lax.map(forward_head, (query_heads, key_heads, value_heads, prior_low))
    attended = heads_last(combined)
    scaled = cotangent.astype(jnp.float32) * gain_wide
    totals = lax.psum(
        (jnp.sum(attended * attended, axis=-1), jnp.sum(scaled * attended, axis=-1)), "tp"
    )
    feature_count = HEADS * HEAD
    inverse = lax.rsqrt(totals[0] / feature_count + epsilon)
    mean_product = totals[1] / feature_count
    normed = (attended * inverse[:, None] * gain_wide).astype(jnp.bfloat16)
    grad_att = (
        inverse[:, None] * scaled - (inverse**3 * mean_product)[:, None] * attended
    ).astype(jnp.bfloat16)
    grad_heads = heads_first(grad_att, head_count)

    def middle_head(members):
        query_now, key_now, value_now, grad_now, prior_now = members
        products = jnp.einsum("te,se->ts", grad_now, value_now, preferred_element_type=jnp.float32)
        cross_low = jnp.where(causal, products, 0.0).astype(jnp.bfloat16)
        grad_query = jnp.dot(cross_low, key_now, preferred_element_type=jnp.float32)
        grad_query = grad_query + jnp.einsum(
            "tf,ef->te", grad_now, prior_now, preferred_element_type=jnp.float32
        )
        later_own = jnp.einsum("te,tf->ef", query_now, grad_now, preferred_element_type=jnp.float32)
        return (cross_low, grad_query.astype(jnp.bfloat16), later_own)

    cross_low, grad_query, later_own = lax.map(
        middle_head, (query_heads, key_heads, value_heads, grad_heads, prior_low)
    )
    position_now = lax.axis_index("ctx")
    pieces = lax.all_gather(later_own[None], "ctx", axis=0, tiled=True)
    shard_index = jnp.arange(pieces.shape[0], dtype=jnp.int32)
    upper_mask = (shard_index > position_now).astype(jnp.float32)
    after_state = jnp.sum(pieces * upper_mask[:, None, None, None], axis=0)
    after_low = after_state.astype(jnp.bfloat16)

    def final_head(members):
        query_now, key_now, value_now, grad_now, masked_now, cross_now, after_now = members
        grad_key = jnp.einsum("st,se->te", cross_now, query_now, preferred_element_type=jnp.float32)
        grad_key = grad_key + jnp.einsum(
            "tf,ef->te", value_now, after_now, preferred_element_type=jnp.float32
        )
        grad_value = jnp.einsum(
            "st,sf->tf", masked_now, grad_now, preferred_element_type=jnp.float32
        )
        grad_value = grad_value + jnp.dot(key_now, after_now, preferred_element_type=jnp.float32)
        return (grad_key.astype(jnp.bfloat16), grad_value.astype(jnp.bfloat16))

    grad_key, grad_value = lax.map(
        final_head, (query_heads, key_heads, value_heads, grad_heads, masked, cross_low, after_low)
    )
    return (normed, heads_last(grad_query), heads_last(grad_key), heads_last(grad_value))


def solution(mesh):
    in_specs = (P("ctx", "tp"), P("ctx", "tp"), P("ctx", "tp"), P("tp"), P("ctx", "tp"))
    out_specs = (P("ctx", "tp"), P("ctx", "tp"), P("ctx", "tp"), P("ctx", "tp"))
    return jax.shard_map(shards, mesh=mesh, in_specs=in_specs, out_specs=out_specs, check_vma=False)
```

profile of v0, /device:TPU:1, one launch (start us, length us, event | category | flops | bytes accessed | tf_op | source)
XLA Modules:
  0.0 234.4 jit_solution(15956539192981530037)
XLA Ops:
  7.2 0.0 all-gather.5.cloned.1.call-start
  7.2 1.1 copy.34
  8.3 1.1 copy.35
  9.4 0.9 fusion.81
  10.3 0.0 all-gather.5.cloned.1.call-update
  10.3 0.0 all-gather.7.cloned.1.call-start
  10.4 0.2 copy.38
  10.5 0.2 copy.39
  10.8 1.1 copy.33
  11.8 0.2 copy.37
  12.0 0.7 convert_element_type.49
  12.7 93.3 %all-gather.5.cloned.1.call-done = f32[128,128,128]{2,1,0:T(8,128)} async-done(((f32[2,128,128]{2,1,0:T(8,128)}), f32[128,128,128]{2,1,0:T(8,128)}) %all-gather.5.cloned.1.call-update) | async-done | bytes 8388624 | tf_op jit(solution)/shard_map/all_gather | solution.py:31
  106.0 4.1 %multiply_reduce_fusion.1 = bf16[2,128,128]{2,1,0:T(8,128)(2,1)S(1)} fusion(f32[64,2,128,128]{3,2,1,0:T(8,128)} %bitcast.213, f32[64]{0:T(128)S(1)} %compare_convert_fusion.1), kind=kLoop, calls=%fused_computation.83 | loop fusion | flops 4161536 | bytes 8454400 | tf_op jit(solution)/shard_map/reduce_sum | solution.py:34
  110.1 0.0 copy-start
  110.1 0.1 broadcast.22.clone
  110.2 1.6 while.41
  110.2 0.3 bitcast_dynamic-update-slice_fusion.4
  110.5 0.3 fusion.134
  110.8 0.2 fusion.135
  111.0 0.3 bitcast_dynamic-update-slice_fusion.4
  111.3 0.3 fusion.134
  111.6 0.2 fusion.135
  111.8 0.1 fusion.78
  112.0 0.0 copy-done
  112.0 0.1 fusion.75
  112.2 14.4 %all-reduce = (f32[512]{0:T(512)S(1)}, f32[512]{0:T(512)S(1)}) all-reduce(f32[512]{0:T(512)S(1)} %fusion.78, f32[512]{0:T(512)S(1)} %fusion.75), channel_id=1, replica_groups=mesh['ctx'=64,'tp'=8] {'tp'}, use_global_device_ids=true, to_apply=%region_4.5 | all-reduce | flops 1024 | bytes 8192 | tf_op jit(solution)/shard_map/psum | solution.py:48
  126.6 0.9 fusion.79
  127.5 0.1 broadcast.22
  127.6 3.4 %while.42 = (s32[]{:T(128)}, bf16[2,512,512]{2,1,0:T(8,128)(2,1)S(1)}, bf16[2,512,128]{2,1,0:T(8,128)(2,1)S(1)}, f32[2,128,128]{2,1,0:T(8,128)}, bf16[2,512,128]...) while((s32[]{:T(128)}, ...), condition=%wide.region_8.9_spmd.clone, body=%wide.region_7.8_spmd.clone.sunk | while | flops 168689664 | bytes 3117673 | solution.py:71
  127.6 0.3 bitcast_dynamic-update-slice_fusion.5
  128.0 0.3 fusion.142
  128.3 0.2 fusion.143
  128.5 0.9 fusion.144
  129.3 0.3 bitcast_dynamic-update-slice_fusion.5
  129.7 0.3 fusion.142
  130.0 0.2 fusion.143
  130.2 0.9 fusion.144
  131.1 0.0 all-gather.7.cloned.1.call-update
  131.1 0.7 copy_bitcast_fusion.2
  131.8 85.6 %all-gather.7.cloned.1.call-done = f32[128,128,128]{2,1,0:T(8,128)} async-done(((f32[2,128,128]{2,1,0:T(8,128)}), f32[128,128,128]{2,1,0:T(8,128)}) %all-gather.7.cloned.1.call-update) | async-done | bytes 8388624 | tf_op jit(solution)/shard_map/all_gather | solution.py:75
  217.5 4.1 %multiply_reduce_fusion = bf16[2,128,128]{2,1,0:T(8,128)(2,1)S(1)} fusion(f32[64,2,128,128]{3,2,1,0:T(8,128)} %bitcast.214, f32[64]{0:T(128)S(1)} %compare_convert_fusion), kind=kLoop, calls=%fused_computation.82 | loop fusion | flops 4161536 | bytes 8454400 | tf_op jit(solution)/shard_map/reduce_sum | solution.py:78
  221.6 0.7 broadcast.24.clone.1
  222.3 3.4 %while.40 = (s32[]{:T(128)}, bf16[2,512,128]{2,1,0:T(8,128)(2,1)S(1)}, bf16[2,512,128]{2,1,0:T(8,128)(2,1)}, bf16[2,512,512]{2,1,0:T(8,128)(2,1)S(1)}, bf16[2,51...) while((s32[]{:T(128)}, ...), condition=%wide.region_11.12_spmd, body=%wide.region_10.11_spmd.sunk | while | flops 168034304 | bytes 2954349 | solution.py:93
  222.3 0.3 fusion.126
  222.7 0.2 fusion.127
  222.9 0.3 fusion.128
  223.2 0.8 fusion.129
  224.1 0.3 fusion.126
  224.4 0.2 fusion.127
  224.6 0.3 fusion.128
  225.0 0.8 fusion.129
  225.8 1.8 copy_bitcast_fusion
  (8 shorter events, 0.1 us)
Async XLA Ops:
  7.2 98.8 %all-gather.5.cloned.1.call-start = ((), (), s32[]{:S(2)}) async-start(), calls=%async_computation | async-start | bytes 8519680 | tf_op jit(solution)/shard_map/all_gather | solution.py:31
  10.3 207.1 %all-gather.7.cloned.1.call-start = ((), (), s32[]{:S(2)}) async-start(), calls=%async_computation.1 | async-start | bytes 8519680 | tf_op jit(solution)/shard_map/all_gather | solution.py:75
  110.1 1.9 copy-start
Sparse Core Ops, SparseCore 0:
  11.9 94.0 all-gather.4
  131.2 86.2 all-gather.6
where the time goes:
time: 235 us; the launch traced here: 234 us
  waiting for transfers between devices  179 us (76%)
  blocking collectives  14.4 us (6%)
  between operations  14.2 us (6%)
  other arithmetic  10.1 us (4%)
  matrix products  9.23 us (4%)
  local copies, waits for them, and re-layouts  7.28 us (3%)
    all_gather x1, waiting for transfers between devices, shards(): pieces = lax.all_gather(own_state[None], 'ctx', axis=0, tiled=True)  93.3 us
    all_gather x1, waiting for transfers between devices, shards(): pieces = lax.all_gather(later_own[None], 'ctx', axis=0, tiled=True)  85.6 us
    psum x1, blocking collectives, shards(): lax.psum((jnp.sum(attended * attended, axis=-1), jnp.sum(scaled * attende...  14.4 us
  transfers between devices with their start and end apart: 2, of which 2 were waited for; matrix products, arithmetic and copies ran while one was open for 1% of the time, Pallas kernels for 0%

commit v1 on v0

--- a/solution.py
+++ b/solution.py
@@ -6,6 +6,13 @@
 HEAD = 128
 HEADS = 16
 epsilon = 1e-06
+
+
+def swapped_in(shard, name, along):
+    devices = lax.axis_size(name)
+    blocks = jnp.stack([shard for _ in range(devices)])
+    blocks = lax.all_to_all(blocks, name, split_axis=0, concat_axis=0)
+    return jnp.concatenate(blocks, axis=along)
 
 
 def heads_first(matrix, head_count):
@@ -28,7 +35,7 @@
         "hte,htf->hef", key_heads, value_heads, preferred_element_type=jnp.float32
     )
     position = lax.axis_index("ctx")
-    pieces = lax.all_gather(own_state[None], "ctx", axis=0, tiled=True)
+    pieces = swapped_in(own_state[None], "ctx", 0)
     shard_index = jnp.arange(pieces.shape[0], dtype=jnp.int32)
     lower_mask = (shard_index < position).astype(jnp.float32)
     prior_state = jnp.sum(pieces * lower_mask[:, None, None, None], axis=0)

time: 235 us -> 344 us (1.46)
  waiting for transfers between devices: 179 us -> 269 us
  starting transfers between devices: 0.08 us -> 12.2 us
  blocking collectives: 14.4 us -> 19.2 us
    all_to_all x0 -> x1, waiting for transfers between devices: none -> 185 us  [swapped_in(): blocks = lax.all_to_all(blocks, name, split_axis=0, concat_axis=0)]
    all_gather x1 -> x0, waiting for transfers between devices: 93.3 us -> none  [shards(): pieces = lax.all_gather(own_state[None], 'ctx', axis=0, tiled=True)]
    all_to_all x0 -> x1, starting transfers between devices: none -> 12.1 us  [swapped_in(): blocks = lax.all_to_all(blocks, name, split_axis=0, concat_axis=0)]
    psum x1, blocking collectives: 14.4 us -> 19.2 us  [shards(): lax.psum((jnp.sum(attended * attended, axis=-1), jnp.sum(scaled * attende...]
    another operation x5 -> x6, local copies, waits for them, and re-layouts: 0.94 us -> 5.21 us  [the longest x1 4.27 us: swapped_in(): blocks = jnp.stack([shard for _ in range(devices)])]
  transfers between devices with their start and end apart: 2 -> 2, of which waited for: 2 -> 2; matrix products, arithmetic and copies ran while one was open for 1% -> 0% of each run, Pallas kernels for 0% -> 0%
where the time goes in v1:
time: 344 us; the launch traced here: 343 us
  waiting for transfers between devices  269 us (78%)
  blocking collectives  19.2 us (6%)
  between operations  14.2 us (4%)
  starting transfers between devices  12.2 us (4%)
  local copies, waits for them, and re-layouts  10.6 us (3%)
  other arithmetic  9.42 us (3%)
  matrix products  8.58 us (2%)
    all_to_all x1, waiting for transfers between devices, swapped_in(): blocks = lax.all_to_all(blocks, name, split_axis=0, concat_axis=0)  185 us
    all_gather x1, waiting for transfers between devices, shards(): pieces = lax.all_gather(later_own[None], 'ctx', axis=0, tiled=True)  83.9 us
    psum x1, blocking collectives, shards(): lax.psum((jnp.sum(attended * attended, axis=-1), jnp.sum(scaled * attende...  19.2 us
    all_to_all x1, starting transfers between devices, swapped_in(): blocks = lax.all_to_all(blocks, name, split_axis=0, concat_axis=0)  12.1 us
  transfers between devices with their start and end apart: 2, of which 2 were waited for; matrix products, arithmetic and copies ran while one was open for 0% of the time, Pallas kernels for 0%

profile of v1, /device:TPU:1, one launch (start us, length us, event | category | flops | bytes accessed | tf_op | source)
XLA Modules:
  0.0 343.3 jit_solution(9231405420322590191)
XLA Ops:
  7.2 1.1 copy.70
  8.3 1.1 copy.71
  9.4 0.2 fusion.82
  9.6 4.3 %stack.3 = f32[64,1,2,128,128]{4,3,2,1,0:T(8,128)} broadcast(f32[2,128,128]{2,1,0:T(8,128)S(1)} %fusion.82), dimensions={2,3,4} | broadcast | bytes 8519680 | tf_op jit(solution)/shard_map/stack | solution.py:13
  13.9 0.0 copy-start.1
  13.9 0.0 copy-start.2
  13.9 12.1 %all-to-all-start = ((f32[64,1,2,128,128]{4,3,2,1,0:T(8,128)}), f32[64,1,2,128,128]{4,3,2,1,0:T(8,128)}, u32[]{:S(2)}, u32[]{:S(2)}) async-start(f32[64,1,2,128,128]{4,3,2,1,0:T(8,128)} %stack.3), calls=%async_computation | async-start | bytes 16777216 | tf_op jit(solution)/shard_map/all_to_all | solution.py:14
  26.0 0.0 all-gather.3.cloned.1.call-start
  26.1 0.2 copy.74
  26.2 0.2 copy.75
  26.4 0.0 copy-done.1
  26.4 0.1 copy.69
  26.6 0.2 copy.73
  26.8 0.0 copy-done.2
  26.8 185.0 %all-to-all-done = f32[64,1,2,128,128]{4,3,2,1,0:T(8,128)} async-done(((f32[64,1,2,128,128]{4,3,2,1,0:T(8,128)}), f32[64,1,2,128,128]{4,3,2,1,0:T(8,128)}, u32[]{:S(2)}, u32[]{:S(2)}) %all-to-all-start) | async-done | bytes 8388640 | tf_op jit(solution)/shard_map/all_to_all | solution.py:14
  211.8 4.1 %fusion.73 = bf16[2,128,128]{2,1,0:T(8,128)(2,1)S(1)} fusion(f32[64,1,2,128,128]{4,3,2,1,0:T(8,128)} %all-to-all-done, f32[64]{0:T(128)S(1)} %compare_convert_fusion.1), kind=kLoop, calls=%fused_computation.83 | loop fusion | flops 4161536 | bytes 8454400 | tf_op jit(solution)/shard_map/reduce_sum | solution.py:41
  215.9 0.0 copy-start
  215.9 0.1 broadcast.24.clone
  216.0 1.6 while.41
  216.0 0.3 bitcast_dynamic-update-slice_fusion.4
  216.3 0.3 fusion.135
  216.6 0.2 fusion.136
  216.8 0.3 bitcast_dynamic-update-slice_fusion.4
  217.1 0.3 fusion.135
  217.4 0.2 fusion.136
  217.6 0.1 fusion.79
  217.8 0.0 copy-done
  217.8 0.1 fusion.76
  218.0 19.2 %all-reduce = (f32[512]{0:T(512)S(1)}, f32[512]{0:T(512)S(1)}) all-reduce(f32[512]{0:T(512)S(1)} %fusion.79, f32[512]{0:T(512)S(1)} %fusion.76), channel_id=1, replica_groups=mesh['ctx'=64,'tp'=8] {'tp'}, use_global_device_ids=true, to_apply=%region_4.5 | all-reduce | flops 1024 | bytes 8192 | tf_op jit(solution)/shard_map/psum | solution.py:55
  237.2 0.9 fusion.80
  238.1 0.1 broadcast.24
  238.2 3.4 while.42
  238.2 0.3 bitcast_dynamic-update-slice_fusion.5
  238.5 0.3 fusion.143
  238.9 0.2 fusion.144
  239.1 0.9 fusion.145
  239.9 0.3 bitcast_dynamic-update-slice_fusion.5
  240.2 0.3 fusion.143
  240.6 0.2 fusion.144
  240.8 0.9 fusion.145
  241.6 0.0 all-gather.3.cloned.1.call-update
  241.7 0.7 copy_bitcast_fusion.2
  242.4 83.9 %all-gather.3.cloned.1.call-done = f32[128,128,128]{2,1,0:T(8,128)} async-done(((f32[2,128,128]{2,1,0:T(8,128)}), f32[128,128,128]{2,1,0:T(8,128)}) %all-gather.3.cloned.1.call-update) | async-done | bytes 8388624 | tf_op jit(solution)/shard_map/all_gather | solution.py:82
  326.3 4.1 %multiply_reduce_fusion = bf16[2,128,128]{2,1,0:T(8,128)(2,1)S(1)} fusion(f32[64,2,128,128]{3,2,1,0:T(8,128)} %bitcast.216, f32[64]{0:T(128)S(1)} %compare_convert_fusion), kind=kLoop, calls=%fused_computation.84 | loop fusion | flops 4161536 | bytes 8454400 | tf_op jit(solution)/shard_map/reduce_sum | solution.py:85
  330.4 0.7 broadcast.26.clone.1
  331.2 3.5 %while.40 = (s32[]{:T(128)}, bf16[2,512,128]{2,1,0:T(8,128)(2,1)S(1)}, bf16[2,512,128]{2,1,0:T(8,128)(2,1)}, bf16[2,512,512]{2,1,0:T(8,128)(2,1)S(1)}, bf16[2,51...) while((s32[]{:T(128)}, ...), condition=%wide.region_11.12_spmd, body=%wide.region_10.11_spmd.sunk | while | flops 168034304 | bytes 2954349 | solution.py:100
  331.2 0.3 fusion.127
  331.5 0.2 fusion.128
  331.7 0.3 fusion.129
  332.1 0.8 fusion.130
  332.9 0.3 fusion.127
  333.2 0.2 fusion.128
  333.5 0.3 fusion.129
  333.8 0.8 fusion.130
  334.6 1.8 copy_bitcast_fusion
  (9 shorter events, 0.1 us)
Async XLA Ops:
  13.9 12.6 %copy-start.1 = (bf16[512,256]{1,0:T(8,128)(2,1)S(1)}, bf16[512,256]{1,0:T(8,128)(2,1)}, u32[]{:S(2)}) copy-start(bf16[512,256]{1,0:T(8,128)(2,1)} %param.11) | copy-start | bytes 786436
  13.9 12.9 %copy-start.2 = (bf16[256]{0:T(256)(128)(2,1)S(1)}, bf16[256]{0:T(256)(128)(2,1)}, u32[]{:S(2)}) copy-start(bf16[256]{0:T(256)(128)(2,1)} %param.14) | copy-start | bytes 1540
  13.9 197.9 %all-to-all-start = ((f32[64,1,2,128,128]{4,3,2,1,0:T(8,128)}), f32[64,1,2,128,128]{4,3,2,1,0:T(8,128)}, u32[]{:S(2)}, u32[]{:S(2)}) async-start(f32[64,1,2,128,128]{4,3,2,1,0:T(8,128)} %stack.3), calls=%async_computation | async-start | bytes 16777216 | tf_op jit(solution)/shard_map/all_to_all | solution.py:14
  26.0 300.3 %all-gather.3.cloned.1.call-start = ((), (), s32[]{:S(2)}) async-start(), calls=%async_computation.1 | async-start | bytes 8519680 | tf_op jit(solution)/shard_map/all_gather | solution.py:82
  215.9 1.9 copy-start
Sparse Core Ops, SparseCore 0:
  241.8 84.4 all-gather.2
